TPU v7x, 768 devices: a whole 4x8x12 slice. The times are simulated.
768 devices in a mesh: tower: 12 (over z), member: 8 (over y), rep: 8 (over x, core).
Axes of the slice: x: 4, y: 8, z: 12, core: 2. Of those that a mesh axis runs over, the one named last changes fastest.
Arguments:
- pooled: bfloat16 [12, 8, 8, 64, 96, 128], P('tower', 'member', 'rep'), may hold values from -6 to 6
- live_count: int32 [12], P('tower'), may hold values from 1 to 8, as said below
- row_map: int32 [8, 8, 768], P('member', 'rep'), may hold values from 0 to 767, as said below
- tower_in: bfloat16 [12, 1024, 512], P('tower'), may hold values from -0.1875 to 0.1875
- bias_in: float32 [12, 512], P('tower'), may hold values from -3 to 3
- tower_out: bfloat16 [12, 512, 288], P('tower'), may hold values from -0.25 to 0.25
- bias_out: float32 [12, 288], P('tower'), may hold values from -3 to 3
- cross_down: bfloat16 [3456, 512], replicated, may hold values from -0.109375 to 0.109375
- cross_up: bfloat16 [512, 3456], replicated, may hold values from -0.25 to 0.25
- cross_bias: float32 [3456], replicated, may hold values from -3 to 3
- grad_out: bfloat16 [8, 8, 768, 3456], P('member', 'rep', 'tower'), may hold values from -6 to 6
Outputs:
- crossed: bfloat16 [8, 8, 768, 3456], P('member', 'rep', 'tower')
- pooled_grad: bfloat16 [12, 8, 8, 64, 96, 128], P('tower', 'member', 'rep')
Inputs may be any that keep to these rules, and one draw needn't show every extreme that they name: Slot k of tower t holds a feature exactly when k < live_count[t]; some tower has 8 live slots and another has 1. `row_map`: for every member and rep index the 768 entries are a permutation of 0 to 767.
All inputs are finite; a program needn't handle non-finite values.
Results may differ from a plain program's by a relative error of at most 0.008.
Values may be sent and summed in bfloat16 or wider, within the bound.
No kernel may reach another device: no remote copies, remote signals or barrier semaphores. Data moves between devices by JAX's collectives and lax.ppermute only.
A program may use at most 64 MiB of HBM per device.

v0:
```python
import jax
import jax.numpy as jnp
from jax import lax
from jax.sharding import PartitionSpec as P


def silu_slope(preact):
    sigma = jax.nn.sigmoid(preact)
    return sigma * (1.0 + preact * (1.0 - sigma))


def on_device(
    pooled,
    live_count,
    row_map,
    tower_in,
    bias_in,
    tower_out,
    bias_out,
    cross_down,
    cross_up,
    cross_bias,
    grad_out,
):
    slot_dev = pooled.shape[1]
    piece_rows = pooled.shape[4]
    emb_width = pooled.shape[5]
    members = lax.axis_size("member")
    replicas = lax.axis_size("rep")
    slot_total = slot_dev * members
    tower_rows = piece_rows * replicas
    received = lax.all_to_all(pooled, ("member", "rep"), split_axis=3, concat_axis=3, tiled=True)
    arranged = jnp.transpose(
        received.reshape(slot_dev, members, replicas, piece_rows, emb_width), (2, 3, 1, 0, 4)
    )
    arranged = arranged.reshape(tower_rows, slot_total * emb_width)
    slot_live = jnp.arange(slot_total, dtype=jnp.int32) < live_count[0]
    column_live = jnp.repeat(slot_live, emb_width)
    inputs = jnp.where(column_live[None, :], arranged, jnp.zeros((), jnp.bfloat16))
    weight_first = tower_in[0]
    weight_second = tower_out[0]
    first_pre = jnp.dot(inputs, weight_first, preferred_element_type=jnp.float32) + bias_in[0]
    hidden = jax.nn.silu(first_pre).astype(jnp.bfloat16)
    second_pre = jnp.dot(hidden, weight_second, preferred_element_type=jnp.float32) + bias_out[0]
    tower_result = jax.nn.silu(second_pre).astype(jnp.bfloat16)
    local_map = row_map[0, 0]
    permuted = jnp.zeros_like(tower_result).at[local_map].set(tower_result)
    joined = lax.all_to_all(permuted, "tower", split_axis=0, concat_axis=1, tiled=True)
    latent = jnp.dot(joined, cross_down, preferred_element_type=jnp.float32).astype(jnp.bfloat16)
    update = jnp.dot(latent, cross_up, preferred_element_type=jnp.float32) + cross_bias
    joined_wide = joined.astype(jnp.float32)
    crossed = (joined_wide + joined_wide * update).astype(jnp.bfloat16)
    cotangent = grad_out[0, 0].astype(jnp.float32)
    scaled = (cotangent * joined_wide).astype(jnp.bfloat16)
    latent_grad = jnp.dot(scaled, cross_up.T, preferred_element_type=jnp.float32).astype(
        jnp.bfloat16
    )
    joined_grad = (
        cotangent * (1.0 + update)
        + jnp.dot(latent_grad, cross_down.T, preferred_element_type=jnp.float32)
    ).astype(jnp.bfloat16)
    returned = lax.all_to_all(joined_grad, "tower", split_axis=1, concat_axis=0, tiled=True)
    out_grad = jnp.take(returned, local_map, axis=0)
    second_grad = (out_grad.astype(jnp.float32) * silu_slope(second_pre)).astype(jnp.bfloat16)
    hidden_grad = jnp.dot(second_grad, weight_second.T, preferred_element_type=jnp.float32)
    first_grad = (hidden_grad * silu_slope(first_pre)).astype(jnp.bfloat16)
    input_grad = jnp.dot(first_grad, weight_first.T, preferred_element_type=jnp.float32)
    input_grad = jnp.where(column_live[None, :], input_grad, 0.0).astype(jnp.bfloat16)
    outgoing = jnp.transpose(
        input_grad.reshape(replicas, piece_rows, members, slot_dev, emb_width), (3, 2, 0, 1, 4)
    )
    outgoing = outgoing.reshape(pooled.shape)
    pooled_grad = lax.all_to_all(
        outgoing, ("member", "rep"), split_axis=3, concat_axis=3, tiled=True
    )
    return (crossed.reshape(grad_out.shape), pooled_grad)


def solution(mesh):
    in_specs = (
        P("tower", "member", "rep", None, None, None),
        P("tower"),
        P("member", "rep", None),
        P("tower", None, None),
        P("tower", None),
        P("tower", None, None),
        P("tower", None),
        P(),
        P(),
        P(),
        P("member", "rep", "tower", None),
    )
    out_specs = (P("member", "rep", "tower", None), P("tower", "member", "rep", None, None, None))
    return jax.shard_map(
        on_device, mesh=mesh, in_specs=in_specs, out_specs=out_specs, check_vma=False
    )
```

profile of v0, /device:TPU:1, one launch (start us, length us, event | category | flops | bytes accessed | tf_op | source)
XLA Modules:
  0.0 219.5 jit_solution(4677312520274640884)
XLA Ops:
  0.6 0.0 copy-start
  0.6 0.0 copy-start.6
  0.7 0.0 copy-start.4
  0.7 15.6 %all-to-all-start = ((bf16[1,1,1,64,96,128]{5,4,2,1,0,3:T(8,128)(2,1)}), bf16[1,1,1,64,96,128]{5,4,2,1,0,3:T(8,128)(2,1)}, u32[]{:S(2)}, u32[]{:S(2)}) async-start(bf16[1,1,1,64,96,128]{5,4,2,1,0,3:T(8,128)(2,1)} %bitcast.64), calls=%async_computation | async-start | bytes 3145728 | tf_op jit(solution)/shard_map/all_to_all | solution.py:32
  17.0 0.0 copy-done.6
  17.0 0.0 copy-done.4
  17.0 0.0 copy-start.7
  17.0 0.0 copy-start.2
  17.1 38.3 %all-to-all-done = bf16[1,1,1,64,96,128]{5,4,2,1,0,3:T(8,128)(2,1)} async-done(((bf16[1,1,1,64,96,128]{5,4,2,1,0,3:T(8,128)(2,1)}), bf16[1,1,1,64,96,128]{5,4,2,1,0,3:T(8,128)(2,1)}, u32[]{:S(2)}, u32[]{:S(2)}) %all-to-all-start) | async-done | bytes 1572896 | tf_op jit(solution)/shard_map/all_to_all | solution.py:32
  55.4 0.0 copy-start.9
  55.4 0.0 copy-start.11
  55.4 2.5 %copy_select_fusion = bf16[1,8,8,96,128]{4,1,3,2,0:T(8,128)(2,1)S(1)} fusion(bf16[1,8,8,96,128]{4,3,2,1,0:T(8,128)(2,1)} %bitcast.3, pred[8]{0:T(512)(128)(4,1)S(1)} %iota_compare_fusion), kind=kLoop, calls=%fused_computation.9 | loop fusion | flops 786432 | bytes 3145736 | tf_op jit(solution)/shard_map/jit(_where)/select_n | solution.py:39
  57.9 0.0 copy-done.7
  57.9 0.0 copy-done.9
  57.9 0.0 copy-done.11
  57.9 0.0 copy-start.10
  57.9 1.0 fusion.5
  58.9 0.0 copy-done.10
  58.9 0.0 copy-start.13
  58.9 1.8 multiply_convert_fusion.3
  60.8 0.0 copy-done.13
  60.8 2.1 copy.24
  62.8 0.0 copy-done.2
  62.8 6.9 %scatter_custom_fusion = bf16[768,288]{1,0:T(8,128)(2,1)} fusion(s32[768]{0:T(1024)S(1)} %fusion.30, bf16[768,288]{1,0:T(8,128)(2,1)} %copy.24, bf16[]{:T(256)} %constant.8.clone.1), kind=kCustom, calls=%fused_computation.35 | custom fusion | bytes 442880 | tf_op jit(solution)/shard_map/scatter | solution.py:47
  69.7 34.6 %all_to_all.48 = bf16[12,64,288]{2,1,0:T(8,128)(2,1)S(1)} all-to-all(bf16[12,64,288]{2,1,0:T(8,128)(2,1)} %bitcast.62), channel_id=1, replica_groups=mesh['tower'=12,'member'=8,'rep'=8] {'tower'}, dimensions={0} | all-to-all | bytes 884736 | tf_op jit(solution)/shard_map/all_to_all | solution.py:48
  104.3 0.0 copy-start.1
  104.3 1.2 copy.25
  105.6 2.4 %all_to_all.38 = bf16[64,3456]{1,0:T(8,128)(2,1)} reshape(bf16[64,12,288]{2,1,0:T(8,128)(2,1)} %copy.25) | data formatting | bytes 884736 | tf_op jit(solution)/shard_map/all_to_all | solution.py:48
  108.0 0.0 copy-done
  108.0 0.0 copy-done.1
  108.0 4.4 %convolution_add_fusion.1 = f32[64,3456]{1,0:T(8,128)} fusion(bf16[512,3456]{1,0:T(8,128)(2,1)S(1)} %copy-done, bf16[64,3456]{1,0:T(8,128)(2,1)} %all_to_all.38, bf16[3456,512]{1,0:T(8,128)(2,1)} %param.18, f32[3456]{0:T(1024)S(1)} %copy-done.1), kind=kOutput, calls=%fused_computation.3 | convolution fusion | flops 453238784 | bytes 8418816 | tf_op jit(solution)/shard_map/dot_general | solution.py:50
  112.4 5.5 %fusion = bf16[64,3456]{1,0:T(8,128)(2,1)} fusion(bf16[3456,512]{1,0:T(8,128)(2,1)} %param.18, bf16[512,3456]{1,0:T(8,128)(2,1)S(1)} %copy-done, f32[64,3456]{1,0:T(8,128)} %convolution_add_fusion.1, bf16[64,3456]{1,0:T(8,128)(2,1)} %all_to_all.38, bf16[1,1,64,3456]{3,2,1,0:T(8,128)(2,1)} %param.21), kind=kOutput, calls=%fused_computation.4 | convolution fusion | flops 455008256 | bytes 9289728 | tf_op jit(solution)/shard_map/dot_general | solution.py:60
  117.8 2.7 %all_to_all.39 = bf16[64,12,288]{2,1,0:T(8,128)(2,1)} reshape(bf16[64,3456]{1,0:T(8,128)(2,1)} %fusion) | data formatting | bytes 884736 | tf_op jit(solution)/shard_map/all_to_all | solution.py:62
  120.5 0.0 copy-start.5
  120.5 0.0 copy-start.3
  120.5 0.0 copy-start.8
  120.5 2.1 copy.26
  122.7 6.2 %all-to-all-start.2 = ((bf16[64,12,288]{2,0,1:T(8,128)(2,1)}), bf16[64,12,288]{2,0,1:T(8,128)(2,1)}, u32[]{:S(2)}, u32[]{:S(2)}) async-start(bf16[64,12,288]{2,0,1:T(8,128)(2,1)} %copy.26), calls=%async_computation.2 | async-start | bytes 1179648 | tf_op jit(solution)/shard_map/all_to_all | solution.py:62
  128.8 0.0 copy-done.5
  128.9 0.0 copy-done.3
  128.9 0.0 copy-done.8
  128.9 0.6 broadcast_bitcast_fusion
  129.5 23.1 %all-to-all-done.2 = bf16[64,12,288]{2,0,1:T(8,128)(2,1)} async-done(((bf16[64,12,288]{2,0,1:T(8,128)(2,1)}), bf16[64,12,288]{2,0,1:T(8,128)(2,1)}, u32[]{:S(2)}, u32[]{:S(2)}) %all-to-all-start.2) | async-done | bytes 442400 | tf_op jit(solution)/shard_map/all_to_all | solution.py:62
  152.6 0.0 copy-start.12
  152.6 4.2 %gather_fusion = bf16[768,288]{1,0:T(8,128)(2,1)} fusion(bf16[768,288]{1,0:T(8,128)(2,1)} %bitcast.15, s32[1024]{0:T(1024)S(1)} %pad_clamp_fusion), kind=kCustom, calls=%fused_computation | custom fusion | bytes 887808 | tf_op jit(solution)/shard_map/jit(_take)/gather | solution.py:63
  156.9 2.0 copy.27
  158.9 0.0 copy-done.12
  158.9 5.2 %fusion.4 = bf16[96,8,8,128]{3,1,2,0:T(8,128)(2,1)} fusion(pred[1024]{0:T(1024)(128)(4,1)S(1)} %copy-done.12, bf16[1,1024,512]{2,1,0:T(8,128)(2,1)} %param.14, f32[768,512]{1,0:T(8,128)} %copy-done.13, f32[768,288]{0,1:T(8,128)} %get-tuple-element.5, bf16[768,288]{0,1:T(8,128)(2,1)} %copy.27, pred[768]{0:T(1024)(128)(4,1)S(1)} %compare_and_fusion, ...), kind=kOutput, calls=%fused_computation.13 | convolution fusion | flops 1039343616 | bytes 5818112 | tf_op jit(solution)/shard_map/dot_general | solution.py:67
  164.2 1.8 copy.31
  166.0 1.4 copy.28
  167.4 10.5 %all-to-all-start.3 = ((bf16[1,1,1,64,96,128]{5,4,2,1,0,3:T(8,128)(2,1)}), bf16[1,1,1,64,96,128]{5,4,2,1,0,3:T(8,128)(2,1)}, u32[]{:S(2)}, u32[]{:S(2)}) async-start(bf16[1,1,1,64,96,128]{5,4,2,1,0,3:T(8,128)(2,1)} %bitcast.60), calls=%async_computation.3 | async-start | bytes 3145728 | tf_op jit(solution)/shard_map/all_to_all | solution.py:73
  177.9 2.1 fusion.14
  180.0 36.8 %all-to-all-done.3 = bf16[1,1,1,64,96,128]{5,4,2,1,0,3:T(8,128)(2,1)} async-done(((bf16[1,1,1,64,96,128]{5,4,2,1,0,3:T(8,128)(2,1)}), bf16[1,1,1,64,96,128]{5,4,2,1,0,3:T(8,128)(2,1)}, u32[]{:S(2)}, u32[]{:S(2)}) %all-to-all-start.3) | async-done | bytes 1572896 | tf_op jit(solution)/shard_map/all_to_all | solution.py:73
  216.9 2.7 %copy.41 = bf16[1,1,1,64,96,128]{5,4,3,2,1,0:T(8,128)(2,1)} copy(bf16[1,1,1,64,96,128]{5,4,3,2,1,0:T(8,128)(2,1)} %bitcast.18) | data formatting | bytes 3145728
  (6 shorter events, 0.1 us)
Async XLA Ops:
  0.6 107.4 %copy-start = (bf16[512,3456]{1,0:T(8,128)(2,1)S(1)}, bf16[512,3456]{1,0:T(8,128)(2,1)}, u32[]{:S(2)}) copy-start(bf16[512,3456]{1,0:T(8,128)(2,1)} %param.19) | copy-start | bytes 10616836
  0.6 16.3 %copy-start.6 = (f32[1,288]{1,0:T(1,128)S(1)}, f32[1,288]{1,0:T(1,128)}, u32[]{:S(2)}) copy-start(f32[1,288]{1,0:T(1,128)} %param.17) | copy-start | bytes 3460
  0.7 16.3 %copy-start.4 = (s32[1,1,768]{2,1,0:T(1,128)S(1)}, s32[1,1,768]{2,1,0:T(1,128)}, u32[]{:S(2)}) copy-start(s32[1,1,768]{2,1,0:T(1,128)} %param.13) | copy-start | bytes 9220
  0.7 54.7 %all-to-all-start = ((bf16[1,1,1,64,96,128]{5,4,2,1,0,3:T(8,128)(2,1)}), bf16[1,1,1,64,96,128]{5,4,2,1,0,3:T(8,128)(2,1)}, u32[]{:S(2)}, u32[]{:S(2)}) async-start(bf16[1,1,1,64,96,128]{5,4,2,1,0,3:T(8,128)(2,1)} %bitcast.64), calls=%async_computation | async-start | bytes 3145728 | tf_op jit(solution)/shard_map/all_to_all | solution.py:32
  17.0 40.9 %copy-start.7 = (pred[8]{0:T(512)(128)(4,1)}, pred[8]{0:T(512)(128)(4,1)S(1)}, u32[]{:S(2)}) copy-start(pred[8]{0:T(512)(128)(4,1)S(1)} %iota_compare_fusion) | copy-start | bytes 28
  17.0 45.8 %copy-start.2 = (s32[768]{0:T(1024)}, s32[768]{0:T(1024)S(1)}, u32[]{:S(2)}) copy-start(s32[768]{0:T(1024)S(1)} %fusion.30) | copy-start | bytes 9220
  55.4 2.5 %copy-start.9 = (bf16[1,1024,512]{2,1,0:T(8,128)(2,1)S(1)}, bf16[1,1024,512]{2,1,0:T(8,128)(2,1)}, u32[]{:S(2)}) copy-start(bf16[1,1024,512]{2,1,0:T(8,128)(2,1)} %param.14) | copy-start | bytes 3145732
  55.4 2.5 %copy-start.11 = (f32[1,512]{1,0:T(1,128)S(1)}, f32[1,512]{1,0:T(1,128)}, u32[]{:S(2)}) copy-start(f32[1,512]{1,0:T(1,128)} %param.15) | copy-start | bytes 6148
  57.9 1.0 copy-start.10
  58.9 1.8 copy-start.13
  104.3 3.7 %copy-start.1 = (f32[3456]{0:T(1024)S(1)}, f32[3456]{0:T(1024)}, u32[]{:S(2)}) copy-start(f32[3456]{0:T(1024)} %param.20) | copy-start | bytes 41476
  120.5 8.3 %copy-start.5 = (s32[1,1,768]{2,1,0:T(1,128)S(1)}, s32[1,1,768]{2,1,0:T(1,128)}, u32[]{:S(2)}) copy-start(s32[1,1,768]{2,1,0:T(1,128)} %param.13) | copy-start | bytes 9220
  120.5 8.3 %copy-start.3 = (s32[768]{0:T(1024)S(1)}, s32[768]{0:T(1024)}, u32[]{:S(2)}) copy-start(s32[768]{0:T(1024)} %copy-done.2) | copy-start | bytes 9220
  120.5 8.3 %copy-start.8 = (pred[8]{0:T(512)(128)(4,1)S(1)}, pred[8]{0:T(512)(128)(4,1)}, u32[]{:S(2)}) copy-start(pred[8]{0:T(512)(128)(4,1)} %copy-done.7) | copy-start | bytes 28
  122.7 30.0 %all-to-all-start.2 = ((bf16[64,12,288]{2,0,1:T(8,128)(2,1)}), bf16[64,12,288]{2,0,1:T(8,128)(2,1)}, u32[]{:S(2)}, u32[]{:S(2)}) async-start(bf16[64,12,288]{2,0,1:T(8,128)(2,1)} %copy.26), calls=%async_computation.2 | async-start | bytes 1179648 | tf_op jit(solution)/shard_map/all_to_all | solution.py:62
  152.6 6.3 %copy-start.12 = (pred[1024]{0:T(1024)(128)(4,1)S(1)}, pred[1024]{0:T(1024)(128)(4,1)}, u32[]{:S(2)}) copy-start(pred[1024]{0:T(1024)(128)(4,1)} %broadcast_bitcast_fusion) | copy-start | bytes 3076
  167.4 49.5 %all-to-all-start.3 = ((bf16[1,1,1,64,96,128]{5,4,2,1,0,3:T(8,128)(2,1)}), bf16[1,1,1,64,96,128]{5,4,2,1,0,3:T(8,128)(2,1)}, u32[]{:S(2)}, u32[]{:S(2)}) async-start(bf16[1,1,1,64,96,128]{5,4,2,1,0,3:T(8,128)(2,1)} %bitcast.60), calls=%async_computation.3 | async-start | bytes 3145728 | tf_op jit(solution)/shard_map/all_to_all | solution.py:73
where the time goes:
time: 220 us
  waiting for transfers between devices  98.3 us (45%)
  blocking collectives  34.6 us (16%)
  starting transfers between devices  32.3 us (15%)
  local copies, waits for them, and re-layouts  30.3 us (14%)
  matrix products  17.8 us (8%)
  other arithmetic  4.72 us (2%)
    all_to_all x1, waiting for transfers between devices, on_device(): lax.all_to_all(pooled, ('member', 'rep'), split_axis=3, concat_axis=3, ti...  38.3 us
    all_to_all x1, waiting for transfers between devices, on_device(): lax.all_to_all(outgoing, ('member', 'rep'), split_axis=3, concat_axis=3,...  36.8 us
    all_to_all x1, blocking collectives, on_device(): lax.all_to_all(permuted, 'tower', split_axis=0, concat_axis=1, tiled=True)  34.6 us
    all_to_all x1, waiting for transfers between devices, on_device(): lax.all_to_all(joined_grad, 'tower', split_axis=1, concat_axis=0, tiled=T...  23.1 us
    all_to_all x1, starting transfers between devices, on_device(): lax.all_to_all(pooled, ('member', 'rep'), split_axis=3, concat_axis=3, ti...  15.6 us
    all_to_all x1, starting transfers between devices, on_device(): lax.all_to_all(outgoing, ('member', 'rep'), split_axis=3, concat_axis=3,...  10.5 us
    scatter x1, local copies, waits for them, and re-layouts, on_device(): permuted = jnp.zeros_like(tower_result).at[local_map].set(tower_result)  6.86 us
    gather x2, local copies, waits for them, and re-layouts, on_device(): out_grad = jnp.take(returned, local_map, axis=0)  6.28 us
  transfers between devices with their start and end apart: 3, of which 3 were waited for; matrix products, arithmetic and copies ran while one was open for 1% of the time, Pallas kernels for 0%

commit v1 on v0

v1 whole, which is shorter than its diff:
```python
import functools

import jax
import jax.numpy as jnp
from jax import lax
from jax.experimental import pallas as pl
from jax.experimental.pallas import tpu as pltpu
from jax.sharding import PartitionSpec as P

BF = jnp.bfloat16
F32 = jnp.float32
LANES = 128
QUAD = 32


def mm(a, b):
    return jnp.dot(a, b, preferred_element_type=F32)


def mm_t(a, b):
    return lax.dot_general(a, b, (((1,), (1,)), ((), ())), preferred_element_type=F32)


def silu(z):
    return z * jax.nn.sigmoid(z)


def silu_slope(z):
    s = jax.nn.sigmoid(z)
    return s * (1.0 + z * (1.0 - s))


def lane_quad(shape):
    return lax.broadcasted_iota(jnp.int32, shape, 1) // QUAD


def prep_body(live_ref, along_ref, down_ref, w1_ref, put_ref, take_ref, w1m_ref):
    rows = put_ref.shape[0]
    put_ref[...] = jnp.where(
        lax.broadcasted_iota(jnp.int32, (rows, rows), 0) == along_ref[...], 1.0, 0.0
    ).astype(BF)
    take_ref[...] = jnp.where(
        lax.broadcasted_iota(jnp.int32, (rows, rows), 1) == down_ref[...], 1.0, 0.0
    ).astype(BF)
    for k in range(w1_ref.shape[0] // LANES):
        rs = slice(k * LANES, (k + 1) * LANES)

        @pl.when(k < live_ref[0])
        def _():
            w1m_ref[rs, :] = w1_ref[rs, :]

        @pl.when(k >= live_ref[0])
        def _():
            w1m_ref[rs, :] = jnp.zeros((LANES, w1_ref.shape[1]), BF)


def forward_body(x_ref, w1_ref, b1_ref, w2_ref, b2_ref, put_ref, out_ref, fp_ref, sp_ref, tr_ref, *, step):
    slots, rows, _ = x_ref.shape
    peers = out_ref.shape[0]
    own = rows // peers
    quarter = own // 4
    for c in range(rows // step):
        rs = slice(c * step, (c + 1) * step)
        x = jnp.concatenate([x_ref[k, rs, :] for k in range(slots)], axis=1)
        fp = mm(x, w1_ref[...]) + b1_ref[...]
        fp_ref[rs, :] = fp
        sp = mm(silu(fp).astype(BF), w2_ref[...]) + b2_ref[...]
        sp_ref[rs, :] = sp
        tr_ref[rs, :] = silu(sp).astype(BF)
    quad = lane_quad((quarter, LANES))
    for c in range(rows // step):
        moved = mm(put_ref[c * step : (c + 1) * step, :], tr_ref[...])
        for s in range(step // own):
            z = c * (step // own) + s
            mine = moved[s * own : (s + 1) * own, :]
            out_ref[z, 0:own, :] = mine[:, 0:LANES].astype(BF)
            out_ref[z, own : 2 * own, :] = mine[:, LANES : 2 * LANES].astype(BF)
            last = mine[:, 2 * LANES :]
            tail = last[0:quarter]
            for j in range(1, 4):
                tail = jnp.where(quad == j, last[j * quarter : (j + 1) * quarter], tail)
            out_ref[z, 2 * own :, :] = tail.astype(BF)


def backward_body(g_ref, take_ref, fp_ref, sp_ref, w1_ref, w2_ref, out_ref, wide_ref, *, step):
    peers = g_ref.shape[0]
    slots, rows, _ = out_ref.shape
    own = rows // peers
    quarter = own // 4
    quad = lane_quad((quarter, LANES))
    for z in range(peers):
        r0 = z * own
        wide_ref[r0 : r0 + own, 0:LANES] = g_ref[z, 0:own, :]
        wide_ref[r0 : r0 + own, LANES : 2 * LANES] = g_ref[z, own : 2 * own, :]
        tail = g_ref[z, 2 * own :, :].astype(F32)
        for j in range(4):
            wide_ref[r0 + j * quarter : r0 + (j + 1) * quarter, 2 * LANES :] = jnp.where(
                quad == j, tail, 0.0
            ).astype(BF)
    for c in range(rows // step):
        rs = slice(c * step, (c + 1) * step)
        og = mm(take_ref[rs, :], wide_ref[...])
        sg = (og * silu_slope(sp_ref[rs, :])).astype(BF)
        hg = mm_t(sg, w2_ref[...])
        fg = (hg * silu_slope(fp_ref[rs, :])).astype(BF)
        ig = mm_t(fg, w1_ref[...])
        for k in range(slots):
            out_ref[k, rs, :] = ig[:, k * LANES : (k + 1) * LANES].astype(BF)


def rolled(v, shift):
    shift %= LANES
    return pltpu.roll(v, shift, 1) if shift else v


def cross_body(j_ref, v_hbm, u_hbm, bias_ref, g_ref, out_ref, crossed_ref,
               v_ref, u_ref, jn_ref, sc_ref, base_ref, jg_ref, sems, *, width, step):
    towers, _, _ = j_ref.shape
    own, total = g_ref.shape
    quarter = own // 4
    get_v = pltpu.make_async_copy(v_hbm, v_ref, sems.at[0])
    get_u = pltpu.make_async_copy(u_hbm, u_ref, sems.at[1])
    get_v.start()
    get_u.start()
    lane = lax.broadcasted_iota(jnp.int32, (own, LANES), 1)
    tiles = [None] * (total // LANES)

    def put(tile, low, high, value):
        held = tiles[tile]
        tiles[tile] = value if held is None else jnp.where((lane >= low) & (lane < high), value, held)

    for t in range(towers):
        first = t * width
        shift = first % LANES
        for h in range(2):
            value = rolled(j_ref[t, h * own : (h + 1) * own, :].astype(F32), shift)
            tile = (first + h * LANES) // LANES
            put(tile, shift, LANES, value)
            if shift:
                put(tile + 1, 0, shift, value)
        start = first + 2 * LANES
        low = start % LANES
        tail = j_ref[t, 2 * own :, :].astype(F32)
        value = jnp.concatenate([rolled(tail, low - j * QUAD) for j in range(4)], axis=0)
        put(start // LANES, low, low + QUAD, value)
    for i, tile in enumerate(tiles):
        cs = slice(i * LANES, (i + 1) * LANES)
        jn_ref[:, cs] = tile.astype(BF)
        sc_ref[:, cs] = (g_ref[:, cs].astype(F32) * tile).astype(BF)
    get_v.wait()
    latent = mm(jn_ref[...], v_ref[...]).astype(BF)
    get_u.wait()
    latent_grad = mm_t(sc_ref[...], u_ref[...]).astype(BF)
    for c in range(total // step):
        cs = slice(c * step, (c + 1) * step)
        update = mm(latent, u_ref[:, cs]) + bias_ref[:, cs]
        j = jn_ref[:, cs].astype(F32)
        crossed_ref[:, cs] = (j + j * update).astype(BF)
        jg_ref[:, cs] = g_ref[:, cs].astype(F32) * (1.0 + update) + mm_t(latent_grad, v_ref[cs, :])
    short = lane_quad((quarter, LANES))
    for t in range(towers):
        first = t * width
        shift = first % LANES
        for h in range(2):
            at = (first + h * LANES) // LANES * LANES
            value = jg_ref[:, at : at + LANES]
            if shift:
                value = jnp.where(lane >= shift, value, jg_ref[:, at + LANES : at + 2 * LANES])
            out_ref[t, h * own : (h + 1) * own, :] = rolled(value, -shift).astype(BF)
        start = first + 2 * LANES
        low = start % LANES
        at = start - low
        tail = None
        for j in range(4):
            value = rolled(jg_ref[j * quarter : (j + 1) * quarter, at : at + LANES], j * QUAD - low)
            tail = value if tail is None else jnp.where(short == j, value, tail)
        out_ref[t, 2 * own :, :] = tail.astype(BF)


def vmem(n):
    return [pl.BlockSpec(memory_space=pltpu.VMEM)] * n


def on_device(pooled, live_count, row_map, tower_in, bias_in, tower_out, bias_out,
              cross_down, cross_up, cross_bias, grad_out):
    groups, piece, emb = pooled.shape[3:]
    slots = lax.axis_size("member")
    reps = lax.axis_size("rep")
    towers = lax.axis_size("tower")
    rows = piece * reps
    own = rows // towers
    hid, width = tower_out.shape[1:]
    rank, total = cross_up.shape
    step = 256 if rows % 256 == 0 else own
    packed = jax.ShapeDtypeStruct((towers, own * width // LANES, LANES), BF)

    received = lax.all_to_all(
        pooled.reshape(groups, piece, emb), ("member", "rep"), split_axis=0, concat_axis=0, tiled=True
    )
    x = received.reshape(slots, rows, emb)

    order = row_map.reshape(rows)
    w1 = tower_in[0]
    put, take, w1m = pl.pallas_call(
        prep_body,
        out_shape=(
            jax.ShapeDtypeStruct((rows, rows), BF),
            jax.ShapeDtypeStruct((rows, rows), BF),
            jax.ShapeDtypeStruct(w1.shape, BF),
        ),
        in_specs=[pl.BlockSpec(memory_space=pltpu.SMEM)] + vmem(3),
        out_specs=tuple(vmem(3)),
        name="prep",
    )(live_count, order.reshape(1, rows), order.reshape(rows, 1), w1)

    def quads(a):
        return jnp.concatenate([a[:, : 2 * LANES]] + [a[:, 2 * LANES :]] * 4, axis=1)

    w2 = quads(tower_out[0])
    b2 = quads(bias_out)
    sent, fp, sp = pl.pallas_call(
        functools.partial(forward_body, step=step),
        out_shape=(
            packed,
            jax.ShapeDtypeStruct((rows, hid), F32),
            jax.ShapeDtypeStruct((rows, 3 * LANES), F32),
        ),
        in_specs=vmem(6),
        out_specs=tuple(vmem(3)),
        scratch_shapes=[pltpu.VMEM((rows, 3 * LANES), BF)],
        name="tower_forward",
    )(x, w1m, bias_in, w2, b2, put)
    joined = lax.all_to_all(sent, "tower", split_axis=0, concat_axis=0, tiled=True)
    joined_grad, crossed = pl.pallas_call(
        functools.partial(cross_body, width=width, step=3 * LANES),
        out_shape=(packed, jax.ShapeDtypeStruct((own, total), BF)),
        in_specs=vmem(1) + [pl.BlockSpec(memory_space=pl.ANY)] * 2 + vmem(2),
        out_specs=tuple(vmem(2)),
        scratch_shapes=[
            pltpu.VMEM((total, rank), BF),
            pltpu.VMEM((rank, total), BF),
            pltpu.VMEM((own, total), BF),
            pltpu.VMEM((own, total), BF),
            pltpu.VMEM((own, total), F32),
            pltpu.VMEM((own, total), F32),
            pltpu.SemaphoreType.DMA((2,)),
        ],
        name="cross",
    )(joined, cross_down, cross_up, cross_bias.reshape(1, total), grad_out.reshape(own, total))
    returned = lax.all_to_all(joined_grad, "tower", split_axis=0, concat_axis=0, tiled=True)
    outgoing = pl.pallas_call(
        functools.partial(backward_body, step=step),
        out_shape=jax.ShapeDtypeStruct((slots, rows, emb), BF),
        in_specs=vmem(6),
        out_specs=vmem(1)[0],
        scratch_shapes=[pltpu.VMEM((rows, 3 * LANES), BF)],
        name="tower_backward",
    )(returned, take, fp, sp, w1m, w2)
    pooled_grad = lax.all_to_all(
        outgoing.reshape(groups, piece, emb), ("member", "rep"), split_axis=0, concat_axis=0, tiled=True
    )
    return (crossed.reshape(grad_out.shape), pooled_grad.reshape(pooled.shape))


def solution(mesh):
    in_specs = (
        P("tower", "member", "rep", None, None, None),
        P("tower"),
        P("member", "rep", None),
        P("tower", None, None),
        P("tower", None),
        P("tower", None, None),
        P("tower", None),
        P(),
        P(),
        P(),
        P("member", "rep", "tower", None),
    )
    out_specs = (P("member", "rep", "tower", None), P("tower", "member", "rep", None, None, None))
    return jax.shard_map(
        on_device, mesh=mesh, in_specs=in_specs, out_specs=out_specs, check_vma=False
    )
```

time: 220 us -> 183 us (0.83)
  waiting for transfers between devices: 98.3 us -> 49.7 us
  blocking collectives: 34.6 us -> 74.4 us
  local copies, waits for them, and re-layouts: 30.3 us -> 4.84 us
  Pallas kernels: 0 us -> 23.8 us
  matrix products: 17.8 us -> 0 us
  starting transfers between devices: 32.3 us -> 26.6 us
  other arithmetic: 4.72 us -> 1.57 us
    all_to_all x3 -> x2, waiting for transfers between devices: 98.3 us -> 49.7 us  [the longest x1 31.7 us: on_device(): lax.all_to_all(pooled.reshape(groups, piece, emb), ('member', 'rep'), spl...]
    all_to_all x1 -> x2, blocking collectives: 34.6 us -> 74.4 us  [the longest x1 48.6 us: on_device(): lax.all_to_all(outgoing.reshape(groups, piece, emb), ('member', 'rep'), s...]
    pallas_call x0 -> x4, Pallas kernels: none -> 23.8 us  [the longest x1 8.03 us: on_device(): pl.pallas_call(functools.partial(cross_body, width=width, step=3 * LANES)...]
    dot_general x5 -> x0, matrix products: 17.8 us -> none  [the longest x1 5.47 us: on_device(): jnp.dot(latent_grad, cross_down.T, preferred_element_type=jnp.float32)]
    all_to_all x4 -> x0, local copies, waits for them, and re-layouts: 8.48 us -> none  [the longest x2 4.81 us: on_device(): lax.all_to_all(joined_grad, 'tower', split_axis=1, concat_axis=0, tiled=T...]
    scatter x1 -> x0, local copies, waits for them, and re-layouts: 6.86 us -> none  [on_device(): permuted = jnp.zeros_like(tower_result).at[local_map].set(tower_result)]
    gather x2 -> x0, local copies, waits for them, and re-layouts: 6.28 us -> none  [on_device(): out_grad = jnp.take(returned, local_map, axis=0)]
    all_to_all x3 -> x2, starting transfers between devices: 32.3 us -> 26.6 us  [the longest x1 14.7 us: on_device(): lax.all_to_all(pooled.reshape(groups, piece, emb), ('member', 'rep'), spl...]
  transfers between devices with their start and end apart: 3 -> 2, of which waited for: 3 -> 2; matrix products, arithmetic and copies ran while one was open for 1% -> 2% of each run, Pallas kernels for 0% -> 2%
where the time goes in v1:
time: 183 us; the launch traced here: 182 us
  blocking collectives  74.4 us (41%)
  waiting for transfers between devices  49.7 us (27%)
  starting transfers between devices  26.6 us (15%)
  Pallas kernels  23.8 us (13%)
  local copies, waits for them, and re-layouts  4.84 us (3%)
    all_to_all x1, blocking collectives, on_device(): lax.all_to_all(outgoing.reshape(groups, piece, emb), ('member', 'rep'), s...  48.6 us
    all_to_all x1, waiting for transfers between devices, on_device(): lax.all_to_all(pooled.reshape(groups, piece, emb), ('member', 'rep'), spl...  31.7 us
    all_to_all x1, blocking collectives, on_device(): lax.all_to_all(joined_grad, 'tower', split_axis=0, concat_axis=0, tiled=T...  25.8 us
    all_to_all x1, waiting for transfers between devices, on_device(): lax.all_to_all(sent, 'tower', split_axis=0, concat_axis=0, tiled=True)  18 us
    all_to_all x1, starting transfers between devices, on_device(): lax.all_to_all(pooled.reshape(groups, piece, emb), ('member', 'rep'), spl...  14.7 us
    all_to_all x1, starting transfers between devices, on_device(): lax.all_to_all(sent, 'tower', split_axis=0, concat_axis=0, tiled=True)  11.8 us
    pallas_call x1, Pallas kernels, on_device(): pl.pallas_call(functools.partial(cross_body, width=width, step=3 * LANES)...  8.03 us
    pallas_call x1, Pallas kernels, on_device(): pl.pallas_call(functools.partial(backward_body, step=step), out_shape=jax...  6.37 us
  transfers between devices with their start and end apart: 2, of which 2 were waited for; matrix products, arithmetic and copies ran while one was open for 2% of the time, Pallas kernels for 2%

profile of v1, /device:TPU:1, one launch (start us, length us, event | category | flops | bytes accessed | tf_op | source)
XLA Modules:
  0.0 182.2 jit_solution(10507562719506252025)
XLA Ops:
  0.6 0.0 copy-start.4
  0.6 0.0 copy-start.2
  0.7 14.7 %all-to-all-start = ((bf16[64,96,128]{2,1,0:T(8,128)(2,1)}), bf16[64,96,128]{2,1,0:T(8,128)(2,1)S(1)}, u32[]{:S(2)}, u32[]{:S(2)}) async-start(bf16[64,96,128]{2,1,0:T(8,128)(2,1)} %bitcast.15), calls=%async_computation | async-start | bytes 3145728 | tf_op jit(solution)/shard_map/all_to_all | solution.py:197
  15.4 0.0 copy-start.5
  15.4 0.0 slice-start
  15.4 0.0 copy-done.4
  15.4 0.9 copy.14.down_ref
  17.0 0.0 copy-done.2
  17.0 0.2 copy.15
  17.3 4.0 %prep.1 = (bf16[768,768]{1,0:T(8,128)(2,1)}, bf16[768,768]{1,0:T(8,128)(2,1)}, bf16[1024,512]{1,0:T(8,128)(2,1)}) custom-call(s32[1]{0:T(128)S(6)} %copy.17.live_ref, s32[1,768]{1,0:T(1,128)} %bitcast.18, s32[768,1]{1,0:T(8,128)} %copy.14.down_ref, bf16[1024,512]{1,0:T(8,128)(2,1)} %bitcast.16), custom_call_target="tpu_custom_call" | custom-call | tf_op jit(solution)/shard_map/prep/pallas_call | solution.py:204
  21.3 0.0 copy-done.5
  21.3 0.0 slice-done
  21.3 0.6 pad_maximum_fusion.1.b2_ref
  21.9 0.9 pad_maximum_fusion.w2_ref
  22.8 31.7 %all-to-all-done = bf16[64,96,128]{2,1,0:T(8,128)(2,1)S(1)} async-done(((bf16[64,96,128]{2,1,0:T(8,128)(2,1)}), bf16[64,96,128]{2,1,0:T(8,128)(2,1)S(1)}, u32[]{:S(2)}, u32[]{:S(2)}) %all-to-all-start) | async-done | bytes 1572896 | tf_op jit(solution)/shard_map/all_to_all | solution.py:197
  54.5 0.0 copy-start
  54.5 1.1 copy-done
  55.7 0.0 copy-start.3
  55.7 5.4 %tower_forward.1 = (bf16[12,144,128]{2,1,0:T(8,128)(2,1)}, f32[768,512]{1,0:T(8,128)}, f32[768,384]{1,0:T(8,128)}) custom-call(bf16[8,768,128]{2,1,0:T(8,128)(2,1)} %bitcast.10, bf16[1024,512]{1,0:T(8,128)(2,1)} %get-tuple-element.10.w1_ref, f32[1,512]{1,0:T(1,128)} %b1_ref.1, bf16[512,384]{1,0:T(8,128)(2,1)} %pad_maximum_fusion.w2_ref, ...), custom_call_target="tpu_custom_call" | custom-call | tf_op jit(solution)/shard_map/tower_forward/pallas_call | solution.py:221
  61.0 11.8 %all-to-all-start.1 = ((bf16[12,144,128]{2,1,0:T(8,128)(2,1)}), bf16[12,144,128]{2,1,0:T(8,128)(2,1)S(1)}, u32[]{:S(2)}, u32[]{:S(2)}) async-start(bf16[12,144,128]{2,1,0:T(8,128)(2,1)} %get-tuple-element.12), calls=%async_computation.1 | async-start | bytes 884736 | tf_op jit(solution)/shard_map/all_to_all | solution.py:233
  72.9 0.0 copy-done.3
  72.9 0.6 reshape.27.bias_ref
  73.5 18.0 %all-to-all-done.1.j_ref = bf16[12,144,128]{2,1,0:T(8,128)(2,1)S(1)} async-done(((bf16[12,144,128]{2,1,0:T(8,128)(2,1)}), bf16[12,144,128]{2,1,0:T(8,128)(2,1)S(1)}, u32[]{:S(2)}, u32[]{:S(2)}) %all-to-all-start.1) | async-done | bytes 442400 | tf_op jit(solution)/shard_map/all_to_all | solution.py:233
  91.5 0.0 copy-start.1
  91.5 0.8 copy-done.1
  92.3 8.0 %cross.1 = (bf16[12,144,128]{2,1,0:T(8,128)(2,1)}, bf16[64,3456]{1,0:T(8,128)(2,1)}) custom-call(bf16[12,144,128]{2,1,0:T(8,128)(2,1)} %copy-done.1, bf16[3456,512]{1,0:T(8,128)(2,1)} %v_hbm.1, bf16[512,3456]{1,0:T(8,128)(2,1)} %u_hbm.1, f32[1,3456]{1,0:T(1,128)} %reshape.27.bias_ref, bf16[64,3456]{1,0:T(8,128)(2,1)} %bitcast.17), custom_call_target="tpu_custom_call" | custom-call | tf_op jit(solution)/shard_map/cross/pallas_call | solution.py:234
  100.3 25.8 %all_to_all.20.g_ref = bf16[12,144,128]{2,1,0:T(8,128)(2,1)} all-to-all(bf16[12,144,128]{2,1,0:T(8,128)(2,1)} %get-tuple-element.14), channel_id=1, replica_groups=mesh['tower'=12,'member'=8,'rep'=8] {'tower'}, dimensions={0} | all-to-all | bytes 884736 | tf_op jit(solution)/shard_map/all_to_all | solution.py:250
  126.1 6.4 %tower_backward.1 = bf16[8,768,128]{2,1,0:T(8,128)(2,1)} custom-call(bf16[12,144,128]{2,1,0:T(8,128)(2,1)} %all_to_all.20.g_ref, bf16[768,768]{1,0:T(8,128)(2,1)} %get-tuple-element.15.take_ref, f32[768,512]{1,0:T(8,128)} %get-tuple-element.16.fp_ref, f32[768,384]{1,0:T(8,128)} %get-tuple-element.17.sp_ref, bf16[1024,512]{1,0:T(8,128)(2,1)} %get-tuple-element.10.w1_ref, ...), custom_call_target="tpu_custom_call" | custom-call | tf_op jit(solution)/shard_map/tower_backward/pallas_call | solution.py:251
  132.5 48.6 %all_to_all.21 = bf16[64,96,128]{2,1,0:T(8,128)(2,1)S(1)} all-to-all(bf16[64,96,128]{2,1,0:T(8,128)(2,1)} %bitcast.11), channel_id=1, replica_groups=mesh['tower'=12,'member'=8,'rep'=8] {'member','rep'}, dimensions={0} | all-to-all | bytes 3145728 | tf_op jit(solution)/shard_map/all_to_all | solution.py:259
  181.1 1.1 copy.18
  (1 shorter events, 0.0 us)
Async XLA Ops:
  0.6 14.8 %copy-start.4 = (s32[1,1,768]{2,1,0:T(1,128)S(1)}, s32[1,1,768]{2,1,0:T(1,128)}, u32[]{:S(2)}) copy-start(s32[1,1,768]{2,1,0:T(1,128)} %param.13) | copy-start | bytes 9220
  0.6 16.4 %copy-start.2 = (bf16[1,512,288]{1,2,0:T(8,128)(2,1)S(1)}, bf16[1,512,288]{1,2,0:T(8,128)(2,1)}, u32[]{:S(2)}) copy-start(bf16[1,512,288]{1,2,0:T(8,128)(2,1)} %param.16) | copy-start | bytes 884740
  0.7 53.9 %all-to-all-start = ((bf16[64,96,128]{2,1,0:T(8,128)(2,1)}), bf16[64,96,128]{2,1,0:T(8,128)(2,1)S(1)}, u32[]{:S(2)}, u32[]{:S(2)}) async-start(bf16[64,96,128]{2,1,0:T(8,128)(2,1)} %bitcast.15), calls=%async_computation | async-start | bytes 3145728 | tf_op jit(solution)/shard_map/all_to_all | solution.py:197
  15.4 5.9 %copy-start.5 = (f32[1,288]{1,0:T(1,128)S(1)}, f32[1,288]{1,0:T(1,128)}, u32[]{:S(2)}) copy-start(f32[1,288]{1,0:T(1,128)} %param.17) | copy-start | bytes 3460
  15.4 5.9 %slice-start = ((f32[1,288]{1,0:T(1,128)}), f32[1,32]{1,0:T(1,128)S(1)}, s32[]{:S(2)}) async-start(f32[1,288]{1,0:T(1,128)} %param.17), calls=%async_computation.4 | async-start | bytes 1024 | tf_op jit(solution)/shard_map/slice | solution.py:217
  54.5 1.1 copy-start
  55.7 17.2 %copy-start.3 = (f32[3456]{0:T(1024)S(1)}, f32[3456]{0:T(1024)}, u32[]{:S(2)}) copy-start(f32[3456]{0:T(1024)} %param.20) | copy-start | bytes 41476
  61.0 30.5 %all-to-all-start.1 = ((bf16[12,144,128]{2,1,0:T(8,128)(2,1)}), bf16[12,144,128]{2,1,0:T(8,128)(2,1)S(1)}, u32[]{:S(2)}, u32[]{:S(2)}) async-start(bf16[12,144,128]{2,1,0:T(8,128)(2,1)} %get-tuple-element.12), calls=%async_computation.1 | async-start | bytes 884736 | tf_op jit(solution)/shard_map/all_to_all | solution.py:233
  91.5 0.8 copy-start.1
